TPU v7x, 32 devices: a whole 2x2x4 slice. The times are simulated.
32 devices in a mesh: trial: 2 (over y), fsdp: 8 (over z, x), tensor: 2 (over core).
Axes of the slice: x: 2, y: 2, z: 4, core: 2. Of those that a mesh axis runs over, the one named last changes fastest.
Arguments:
- tokens: bfloat16 [4096, 4096], P(('trial', 'fsdp'), 'tensor'), parts along dimension 0, may hold values from -110 to 110
- norm_gain: float32 [4096], replicated, may hold values from 0.25 to 1.75
- grow_width: bfloat16 [4096, 2048], P('fsdp'), may hold values from -0.09375 to 0.09375
- old_value: bfloat16 [2048, 1024], P('fsdp', 'tensor'), may hold values from -0.125 to 0.125
- grow_head: bfloat16 [2048, 1024], P('tensor', 'fsdp'), may hold values from -0.1875 to 0.1875
- cotangent: bfloat16 [4096, 2048], P(('trial', 'fsdp'), 'tensor'), parts along dimension 0, may hold values from -6 to 6
Outputs:
- grown_value: bfloat16 [8192, 1024], P(('trial', 'fsdp'), 'tensor'), parts along dimension 0
- value_out: bfloat16 [4096, 2048], P(('trial', 'fsdp'), 'tensor'), parts along dimension 0
- head_grad: float32 [2048, 2048], P(('trial', 'fsdp'), 'tensor'), parts along dimension 0
There are 2 independent parts, one for each index of `trial`. A program takes and returns all parts, laid end to end along the dimension named above; an argument that names none is the same for every part. Nothing has to cross between parts.
All inputs are finite; a program needn't handle non-finite values.
Results may differ from a plain program's by a relative error of at most 0.0064.
Values may be sent and summed in bfloat16 or wider, within the bound.
A program may use at most 64 MiB of HBM per device.

v0:
```python
import math
import jax
import jax.numpy as jnp
from jax import lax
from jax.sharding import PartitionSpec as P


def per_device(tokens, norm_gain, grow_width, old_value, grow_head, cotangent):
    whole = lax.all_gather(tokens, "tensor", axis=1, tiled=True)
    widened = whole.astype(jnp.float32)
    meansq = jnp.mean(widened * widened, axis=-1, keepdims=True)
    normed = (widened * lax.rsqrt(meansq + 1e-05) * norm_gain).astype(jnp.bfloat16)
    old_rows = lax.all_gather(old_value, "tensor", axis=1, tiled=True)
    old_all = lax.all_gather(old_rows, "fsdp", axis=0, tiled=True)
    grown_slab = jnp.dot(grow_width, old_all, preferred_element_type=jnp.float32).astype(
        jnp.bfloat16
    )
    grown_full = lax.all_gather(grown_slab, "fsdp", axis=0, tiled=True)
    mixed = jnp.dot(normed, grown_full, preferred_element_type=jnp.float32).astype(jnp.bfloat16)
    half_width = old_all.shape[1] // lax.axis_size("tensor")
    grown_value = lax.dynamic_slice_in_dim(
        grown_slab, lax.axis_index("tensor") * half_width, half_width, 1
    )
    head_all = lax.all_gather(grow_head, "fsdp", axis=1, tiled=True)
    value_out = lax.dot_general(
        mixed, head_all, (((1,), (1,)), ((), ())), preferred_element_type=jnp.float32
    ).astype(jnp.bfloat16)
    summed = lax.psum_scatter(
        lax.dot_general(
            mixed, cotangent, (((0,), (0,)), ((), ())), preferred_element_type=jnp.float32
        ),
        "fsdp",
        scatter_dimension=0,
        tiled=True,
    )
    head_grad = summed * (1.0 / math.sqrt(tokens.shape[0] * lax.axis_size("fsdp")))
    return (grown_value, value_out, head_grad)


def solution(mesh):
    return jax.shard_map(
        per_device,
        mesh=mesh,
        in_specs=(
            P(("trial", "fsdp"), "tensor"),
            P(),
            P("fsdp", None),
            P("fsdp", "tensor"),
            P("tensor", "fsdp"),
            P(("trial", "fsdp"), "tensor"),
        ),
        out_specs=(
            P(("trial", "fsdp"), "tensor"),
            P(("trial", "fsdp"), "tensor"),
            P(("trial", "fsdp"), "tensor"),
        ),
        check_vma=False,
    )
```

profile of v0, /device:TPU:0, one launch (start us, length us, event | category | flops | bytes accessed | tf_op | source)
XLA Modules:
  0.0 375.4 jit_solution(16384810196821062314)
XLA Ops:
  7.2 0.0 copy-start
  7.2 0.0 all-gather.5.cloned.1.call-start
  7.2 4.3 %all_gather.15 = bf16[256,1024]{1,0:T(8,128)(2,1)} all-gather(bf16[256,512]{1,0:T(8,128)(2,1)} %param.9), channel_id=1, replica_groups=mesh['trial'=2,'fsdp'=8,'tensor'=2] {'tensor'}, dimensions={1}, use_global_device_ids=true | all-gather | bytes 786432 | tf_op jit(solution)/shard_map/all_gather | solution.py:13
  11.6 0.0 all-gather.5.cloned.1.call-update
  11.6 0.0 all-gather.7.cloned.1.call-start
  11.6 0.7 all-gather.7.cloned.1.call-update
  12.3 0.0 copy-start.4
  12.3 0.0 all-gather.9.cloned.1.call-start
  12.4 75.1 %all-gather.5.cloned.1.call-done = bf16[2048,1024]{1,0:T(8,128)(2,1)} async-done(((bf16[256,1024]{1,0:T(8,128)(2,1)}), bf16[2048,1024]{1,0:T(8,128)(2,1)}) %all-gather.5.cloned.1.call-update) | async-done | bytes 4194320 | tf_op jit(solution)/shard_map/all_gather | solution.py:14
  87.5 0.0 copy-done
  87.5 5.6 %convolution_convert_fusion = bf16[512,1024]{1,0:T(8,128)(2,1)} fusion(bf16[512,2048]{1,0:T(8,128)(2,1)S(1)} %copy-done, bf16[2048,1024]{1,0:T(8,128)(2,1)} %all-gather.5.cloned.1.call-done), kind=kOutput, calls=%fused_computation.8 | convolution fusion | flops 2148007936 | bytes 7340032 | tf_op jit(solution)/shard_map/dot_general | solution.py:15
  93.1 0.0 all-gather.9.cloned.1.call-update
  93.1 0.0 all-gather.11.cloned.1.call-start
  93.2 0.5 all-gather.11.cloned.1.call-update
  93.7 0.0 reduce-scatter.2.cloned.1.call-start
  93.7 4.2 %all-gather.7.cloned.1.call-done = bf16[256,4096]{1,0:T(8,128)(2,1)} async-done(((bf16[256,2048]{1,0:T(8,128)(2,1)}), bf16[256,4096]{1,0:T(8,128)(2,1)}) %all-gather.7.cloned.1.call-update) | async-done | bytes 2097168 | tf_op jit(solution)/shard_map/all_gather | solution.py:9
  97.9 2.1 fusion
  100.0 0.0 copy-start.3
  100.0 126.2 %all-gather.9.cloned.1.call-done = bf16[4096,1024]{1,0:T(8,128)(2,1)} async-done(((bf16[512,1024]{1,0:T(8,128)(2,1)}), bf16[4096,1024]{1,0:T(8,128)(2,1)}) %all-gather.9.cloned.1.call-update) | async-done | bytes 8388624 | tf_op jit(solution)/shard_map/all_gather | solution.py:18
  226.2 0.0 copy-done.4
  226.2 6.4 %fusion.7 = bf16[256,1024]{1,0:T(8,128)(2,1)S(1)} fusion(bf16[4096,1024]{1,0:T(8,128)(2,1)} %all-gather.9.cloned.1.call-done, bf16[256,4096]{1,0:T(8,128)(2,1)} %all-gather.7.cloned.1.call-done, f32[4096]{0:T(1024)S(1)} %copy-done.4, f32[256]{0:T(256)S(1)} %add_rsqrt_fusion), kind=kOutput, calls=%fused_computation.9 | convolution fusion | flops 2151940096 | bytes 11027456 | tf_op jit(solution)/shard_map/dot_general | solution.py:19
  232.6 0.0 copy-start.2
  232.6 0.8 copy-done.2
  233.4 0.0 copy-done.3
  233.4 2.7 fusion.10
  236.1 0.0 copy-start.1
  236.1 0.0 reduce-scatter.2.cloned.1.call-update
  236.1 1.2 copy-done.1
  237.3 0.8 constant_dynamic-slice_fusion
  238.2 39.2 %all-gather.11.cloned.1.call-done = bf16[1024,1024]{1,0:T(8,128)(2,1)} async-done(((bf16[1024,128]{1,0:T(8,128)(2,1)}), bf16[1024,1024]{1,0:T(8,128)(2,1)}) %all-gather.11.cloned.1.call-update) | async-done | bytes 2097168 | tf_op jit(solution)/shard_map/all_gather | solution.py:24
  277.4 3.3 convolution_convert_fusion.1
  280.7 86.3 %reduce-scatter.2.cloned.1.call-done = f32[128,1024]{1,0:T(8,128)} async-done(((f32[1024,1024]{1,0:T(8,128)}), f32[128,1024]{1,0:T(8,128)}) %reduce-scatter.2.cloned.1.call-update) | async-done | bytes 524304 | tf_op jit(solution)/shard_map/reduce_scatter | solution.py:28
  367.0 1.9 broadcast_multiply_fusion
  (1 shorter events, 0.0 us)
Async XLA Ops:
  7.2 80.4 %copy-start = (bf16[512,2048]{1,0:T(8,128)(2,1)S(1)}, bf16[512,2048]{1,0:T(8,128)(2,1)}, u32[]{:S(2)}) copy-start(bf16[512,2048]{1,0:T(8,128)(2,1)} %param.8) | copy-start | bytes 6291460
  7.2 80.3 %all-gather.5.cloned.1.call-start = ((), (), s32[]{:S(2)}) async-start(), calls=%async_computation.1 | async-start | bytes 4718592 | tf_op jit(solution)/shard_map/all_gather | solution.py:14
  11.6 86.4 %all-gather.7.cloned.1.call-start = ((), (), s32[]{:S(2)}) async-start(), calls=%async_computation.2 | async-start | bytes 3145728 | tf_op jit(solution)/shard_map/all_gather | solution.py:9
  12.3 213.9 %copy-start.4 = (f32[4096]{0:T(1024)S(1)}, f32[4096]{0:T(1024)}, u32[]{:S(2)}) copy-start(f32[4096]{0:T(1024)} %param.7) | copy-start | bytes 49156
  12.3 213.9 %all-gather.9.cloned.1.call-start = ((), (), s32[]{:S(2)}) async-start(), calls=%async_computation.3 | async-start | bytes 9437184 | tf_op jit(solution)/shard_map/all_gather | solution.py:18
  93.1 184.3 %all-gather.11.cloned.1.call-start = ((), (), s32[]{:S(2)}) async-start(), calls=%async_computation.4 | async-start | bytes 2359296 | tf_op jit(solution)/shard_map/all_gather | solution.py:24
  93.7 273.3 %reduce-scatter.2.cloned.1.call-start = ((), (), s32[]{:S(2)}) async-start(), calls=%async_computation.5 | async-start | bytes 4718592 | tf_op jit(solution)/shard_map/reduce_scatter | solution.py:28
  100.0 133.4 %copy-start.3 = (bf16[256,1024]{1,0:T(8,128)(2,1)S(1)}, bf16[256,1024]{1,0:T(8,128)(2,1)}, u32[]{:S(2)}) copy-start(bf16[256,1024]{1,0:T(8,128)(2,1)} %param.11) | copy-start | bytes 1572868
  232.6 0.8 copy-start.2
  236.1 1.2 copy-start.1
Sparse Core Ops, SparseCore 0:
  11.7 75.7 all-gather.4
  89.1 8.8 all-gather.6
  100.1 126.0 all-gather.8
  228.1 49.2 all-gather.10
  280.9 86.0 reduce-scatter.1
where the time goes:
time: 376 us; the launch traced here: 375 us
  waiting for transfers between devices  332 us (88%)
  matrix products  18 us (5%)
  between operations  13.8 us (4%)
  blocking collectives  4.33 us (1%)
  other arithmetic  3.98 us (1%)
    all_gather x1, waiting for transfers between devices, per_device(): grown_full = lax.all_gather(grown_slab, 'fsdp', axis=0, tiled=True)  126 us
    reduce_scatter x1, waiting for transfers between devices, per_device(): lax.psum_scatter(lax.dot_general(mixed, cotangent, (((0,), (0,)), ((), ()...  86.3 us
    all_gather x1, waiting for transfers between devices, per_device(): old_all = lax.all_gather(old_rows, 'fsdp', axis=0, tiled=True)  75.1 us
    all_gather x1, waiting for transfers between devices, per_device(): head_all = lax.all_gather(grow_head, 'fsdp', axis=1, tiled=True)  39.2 us
  transfers between devices with their start and end apart: 5, of which 5 were waited for; matrix products, arithmetic and copies ran while one was open for 6% of the time, Pallas kernels for 0%

commit v1 on v0

--- a/solution.py
+++ b/solution.py
@@ -15,7 +15,12 @@
     grown_slab = jnp.dot(grow_width, old_all, preferred_element_type=jnp.float32).astype(
         jnp.bfloat16
     )
-    grown_full = lax.all_gather(grown_slab, "fsdp", axis=0, tiled=True)
+    ring = [grown_slab]
+    for hop in range(7):
+        ring.append(lax.ppermute(ring[-1], "fsdp", [(dev, (dev + 1) % 8) for dev in range(8)]))
+    grown_full = jnp.roll(
+        jnp.concatenate(ring[::-1], axis=0), (lax.axis_index("fsdp") + 1) * ring[0].shape[0], axis=0
+    )
     mixed = jnp.dot(normed, grown_full, preferred_element_type=jnp.float32).astype(jnp.bfloat16)
     half_width = old_all.shape[1] // lax.axis_size("tensor")
     grown_value = lax.dynamic_slice_in_dim(

time: 376 us -> 398 us (1.059)
  local copies, waits for them, and re-layouts: 2.83 us -> 19.3 us
  waiting for transfers between devices: 332 us -> 340 us
  matrix products: 18 us -> 12.9 us
    ppermute x0 -> x7, waiting for transfers between devices: none -> 172 us  [per_device(): lax.ppermute(ring[-1], 'fsdp', [(dev, (dev + 1) % 8) for dev in range(8)])]
    all_gather x1 -> x0, waiting for transfers between devices: 126 us -> none  [per_device(): grown_full = lax.all_gather(grown_slab, 'fsdp', axis=0, tiled=True)]
    all_gather x1, waiting for transfers between devices: 39.2 us -> 5.73 us  [per_device(): head_all = lax.all_gather(grow_head, 'fsdp', axis=1, tiled=True)]
    unnamed x10 -> x37, local copies, waits for them, and re-layouts: 2 us -> 18.4 us
    all_gather x1, waiting for transfers between devices: 4.2 us -> 0.03 us  [per_device(): whole = lax.all_gather(tokens, 'tensor', axis=1, tiled=True)]
  transfers between devices with their start and end apart: 5 -> 11, of which waited for: 5 -> 10; matrix products, arithmetic and copies ran while one was open for 6% -> 7% of each run, Pallas kernels for 0% -> 0%
where the time goes in v1:
time: 398 us; the launch traced here: 397 us
  waiting for transfers between devices  340 us (85%)
  local copies, waits for them, and re-layouts  19.3 us (5%)
  between operations  15.9 us (4%)
  matrix products  12.9 us (3%)
  blocking collectives  4.3 us (1%)
  other arithmetic  4.13 us (1%)
    ppermute x7, waiting for transfers between devices, per_device(): lax.ppermute(ring[-1], 'fsdp', [(dev, (dev + 1) % 8) for dev in range(8)])  172 us
    reduce_scatter x1, waiting for transfers between devices, per_device(): lax.psum_scatter(lax.dot_general(mixed, cotangent, (((0,), (0,)), ((), ()...  86.2 us
    all_gather x1, waiting for transfers between devices, per_device(): old_all = lax.all_gather(old_rows, 'fsdp', axis=0, tiled=True)  75.9 us
    unnamed x37, local copies, waits for them, and re-layouts  18.4 us
  transfers between devices with their start and end apart: 11, of which 10 were waited for; matrix products, arithmetic and copies ran while one was open for 7% of the time, Pallas kernels for 0%

profile of v1, /device:TPU:0, one launch (start us, length us, event | category | flops | bytes accessed | tf_op | source)
XLA Modules:
  0.0 397.3 jit_solution(7949012790039925807)
XLA Ops:
  8.0 0.0 copy-start
  8.0 0.0 all-gather.4.cloned.1.call-start
  8.1 4.3 %all_gather.12 = bf16[256,1024]{1,0:T(8,128)(2,1)} all-gather(bf16[256,512]{1,0:T(8,128)(2,1)} %param.9), channel_id=1, replica_groups=mesh['trial'=2,'fsdp'=8,'tensor'=2] {'tensor'}, dimensions={1}, use_global_device_ids=true | all-gather | bytes 786432 | tf_op jit(solution)/shard_map/all_gather | solution.py:13
  12.4 0.0 all-gather.4.cloned.1.call-update
  12.4 0.0 all-gather.6.cloned.1.call-start
  12.4 75.9 %all-gather.4.cloned.1.call-done = bf16[2048,1024]{1,0:T(8,128)(2,1)} async-done(((bf16[256,1024]{1,0:T(8,128)(2,1)}), bf16[2048,1024]{1,0:T(8,128)(2,1)}) %all-gather.4.cloned.1.call-update) | async-done | bytes 4194320 | tf_op jit(solution)/shard_map/all_gather | solution.py:14
  88.4 0.0 copy-done
  88.4 4.5 %convolution_convert_fusion = bf16[512,1024]{1,0:T(8,128)(2,1)S(1)} fusion(bf16[512,2048]{1,0:T(8,128)(2,1)S(1)} %copy-done, bf16[2048,1024]{1,0:T(8,128)(2,1)} %all-gather.4.cloned.1.call-done), kind=kOutput, calls=%fused_computation.9 | convolution fusion | flops 2148007936 | bytes 7340032 | tf_op jit(solution)/shard_map/dot_general | solution.py:15
  92.9 0.6 collective-permute-start
  93.5 25.9 %collective-permute-done = bf16[512,1024]{1,0:T(8,128)(2,1)S(1)} collective-permute-done((bf16[512,1024]{1,0:T(8,128)(2,1)S(1)}, bf16[512,1024]{1,0:T(8,128)(2,1)S(1)}, u32[]{:S(2)}, u32[]{:S(2)}) %collective-permute-start) | collective-permute-done | bytes 1048608 | tf_op jit(solution)/shard_map/ppermute | solution.py:20
  119.4 1.0 copy-done.1
  120.3 0.0 collective-permute-start.1
  120.3 25.5 %collective-permute-done.1 = bf16[512,1024]{1,0:T(8,128)(2,1)S(1)} collective-permute-done((bf16[512,1024]{1,0:T(8,128)(2,1)S(1)}, bf16[512,1024]{1,0:T(8,128)(2,1)S(1)}, u32[]{:S(2)}, u32[]{:S(2)}) %collective-permute-start.1) | collective-permute-done | bytes 1048608 | tf_op jit(solution)/shard_map/ppermute | solution.py:20
  145.8 1.0 copy-done.3
  146.8 0.0 collective-permute-start.2
  146.8 24.6 %collective-permute-done.2 = bf16[512,1024]{1,0:T(8,128)(2,1)S(1)} collective-permute-done((bf16[512,1024]{1,0:T(8,128)(2,1)S(1)}, bf16[512,1024]{1,0:T(8,128)(2,1)S(1)}, u32[]{:S(2)}, u32[]{:S(2)}) %collective-permute-start.2) | collective-permute-done | bytes 1048608 | tf_op jit(solution)/shard_map/ppermute | solution.py:20
  171.4 1.0 copy-done.5
  172.3 0.0 collective-permute-start.3
  172.4 23.7 %collective-permute-done.3 = bf16[512,1024]{1,0:T(8,128)(2,1)} collective-permute-done((bf16[512,1024]{1,0:T(8,128)(2,1)S(1)}, bf16[512,1024]{1,0:T(8,128)(2,1)}, u32[]{:S(2)}, u32[]{:S(2)}) %collective-permute-start.3) | collective-permute-done | bytes 1048608 | tf_op jit(solution)/shard_map/ppermute | solution.py:20
  196.1 0.0 collective-permute-start.4
  196.1 0.0 all-gather.6.cloned.1.call-update
  196.1 0.0 all-gather.8.cloned.1.call-start
  196.2 23.2 %collective-permute-done.4 = bf16[512,1024]{1,0:T(8,128)(2,1)} collective-permute-done((bf16[512,1024]{1,0:T(8,128)(2,1)}, bf16[512,1024]{1,0:T(8,128)(2,1)}, u32[]{:S(2)}, u32[]{:S(2)}) %collective-permute-start.4) | collective-permute-done | bytes 1048608 | tf_op jit(solution)/shard_map/ppermute | solution.py:20
  219.4 0.0 collective-permute-start.5
  219.4 23.3 %collective-permute-done.5 = bf16[512,1024]{1,0:T(8,128)(2,1)} collective-permute-done((bf16[512,1024]{1,0:T(8,128)(2,1)}, bf16[512,1024]{1,0:T(8,128)(2,1)}, u32[]{:S(2)}, u32[]{:S(2)}) %collective-permute-start.5) | collective-permute-done | bytes 1048608 | tf_op jit(solution)/shard_map/ppermute | solution.py:20
  242.7 0.0 collective-permute-start.6
  242.8 0.0 all-gather.8.cloned.1.call-update
  242.8 0.0 reduce-scatter.2.cloned.1.call-start
  242.8 0.0 all-gather.6.cloned.1.call-done
  242.9 0.0 copy-start.6
  242.9 0.0 copy-start.4
  242.9 0.0 copy-start.2
  242.9 2.2 fusion.2
  245.2 0.0 copy-start.10
  245.2 25.7 %collective-permute-done.6 = bf16[512,1024]{1,0:T(8,128)(2,1)} collective-permute-done((bf16[512,1024]{1,0:T(8,128)(2,1)}, bf16[512,1024]{1,0:T(8,128)(2,1)}, u32[]{:S(2)}, u32[]{:S(2)}) %collective-permute-start.6) | collective-permute-done | bytes 1048608 | tf_op jit(solution)/shard_map/ppermute | solution.py:20
  270.9 1.3 constant_dynamic-update-slice_fusion.15
  272.2 1.3 constant_dynamic-update-slice_fusion.14
  273.5 1.3 constant_dynamic-update-slice_fusion.13
  274.8 1.3 constant_dynamic-update-slice_fusion.12
  276.1 1.3 constant_dynamic-update-slice_fusion.11
  277.4 1.3 constant_dynamic-update-slice_fusion.10
  278.7 1.3 constant_dynamic-update-slice_fusion.9
  280.0 0.0 copy-start.9
  280.1 0.1 constant_dynamic-update-slice_fusion.8
  280.1 1.3 constant_dynamic-update-slice_fusion.7
  281.5 1.3 constant_dynamic-update-slice_fusion.6
  282.8 1.3 constant_dynamic-update-slice_fusion.5
  284.1 1.3 constant_dynamic-update-slice_fusion.4
  285.4 0.0 copy-done.6
  285.4 0.1 constant_dynamic-update-slice_fusion.3
  285.5 0.0 copy-done.4
  285.5 0.1 constant_dynamic-update-slice_fusion.2
  285.6 0.1 constant_dynamic-update-slice_fusion.1
  285.6 0.1 constant_dynamic-update-slice_fusion
  285.7 2.4 fusion.8
  288.2 0.0 copy-start.8
  288.2 0.8 copy-done.8
  289.0 2.7 fusion.14
  291.7 0.0 reduce-scatter.2.cloned.1.call-update
  291.7 0.8 constant_dynamic-slice_fusion
  292.5 5.7 %all-gather.8.cloned.1.call-done = bf16[1024,1024]{1,0:T(8,128)(2,1)} async-done(((bf16[1024,128]{1,0:T(8,128)(2,1)}), bf16[1024,1024]{1,0:T(8,128)(2,1)}) %all-gather.8.cloned.1.call-update) | async-done | bytes 2097168 | tf_op jit(solution)/shard_map/all_gather | solution.py:29
  298.3 3.3 convolution_convert_fusion.1
  301.6 86.2 %reduce-scatter.2.cloned.1.call-done = f32[128,1024]{1,0:T(8,128)} async-done(((f32[1024,1024]{1,0:T(8,128)}), f32[128,1024]{1,0:T(8,128)}) %reduce-scatter.2.cloned.1.call-update) | async-done | bytes 524304 | tf_op jit(solution)/shard_map/reduce_scatter | solution.py:33
  387.8 1.9 broadcast_multiply_fusion
  (9 shorter events, 0.0 us)
Async XLA Ops:
  8.0 80.4 %copy-start = (bf16[512,2048]{1,0:T(8,128)(2,1)S(1)}, bf16[512,2048]{1,0:T(8,128)(2,1)}, u32[]{:S(2)}) copy-start(bf16[512,2048]{1,0:T(8,128)(2,1)} %param.8) | copy-start | bytes 6291460
  8.0 80.3 %all-gather.4.cloned.1.call-start = ((), (), s32[]{:S(2)}) async-start(), calls=%async_computation.1 | async-start | bytes 4718592 | tf_op jit(solution)/shard_map/all_gather | solution.py:14
  12.4 230.5 %all-gather.6.cloned.1.call-start = ((), (), s32[]{:S(2)}) async-start(), calls=%async_computation.2 | async-start | bytes 3145728 | tf_op jit(solution)/shard_map/all_gather | solution.py:9
  92.9 26.5 %collective-permute-start = (bf16[512,1024]{1,0:T(8,128)(2,1)S(1)}, bf16[512,1024]{1,0:T(8,128)(2,1)S(1)}, u32[]{:S(2)}, u32[]{:S(2)}) collective-permute-start(bf16[512,1024]{1,0:T(8,128)(2,1)S(1)} %convolution_convert_fusion), channel_id=1, source_target_pairs={{0,2},{2,4},{4,6},{6,8},{8,10},{10,12},{12,14},{14,0},{1,3},{3,5},... | collective-permute-start | bytes 3145736 | tf_op jit(solution)/shard_map/ppermute | solution.py:20
  119.3 1.0 copy-start.1
  120.3 25.5 %collective-permute-start.1 = (bf16[512,1024]{1,0:T(8,128)(2,1)S(1)}, bf16[512,1024]{1,0:T(8,128)(2,1)S(1)}, u32[]{:S(2)}, u32[]{:S(2)}) collective-permute-start(bf16[512,1024]{1,0:T(8,128)(2,1)S(1)} %collective-permute-done), channel_id=1, source_target_pairs={{0,2},{2,4},{4,6},{6,8},{8,10},{10,12},{12,14},{14,0},{1,3},{3,5},... | collective-permute-start | bytes 3145736 | tf_op jit(solution)/shard_map/ppermute | solution.py:20
  145.8 1.0 copy-start.3
  146.8 24.6 %collective-permute-start.2 = (bf16[512,1024]{1,0:T(8,128)(2,1)S(1)}, bf16[512,1024]{1,0:T(8,128)(2,1)S(1)}, u32[]{:S(2)}, u32[]{:S(2)}) collective-permute-start(bf16[512,1024]{1,0:T(8,128)(2,1)S(1)} %collective-permute-done.1), channel_id=1, source_target_pairs={{0,2},{2,4},{4,6},{6,8},{8,10},{10,12},{12,14},{14,0},{1,3},{3,5},... | collective-permute-start | bytes 3145736 | tf_op jit(solution)/shard_map/ppermute | solution.py:20
  171.4 1.0 copy-start.5
  172.3 23.8 %collective-permute-start.3 = (bf16[512,1024]{1,0:T(8,128)(2,1)S(1)}, bf16[512,1024]{1,0:T(8,128)(2,1)}, u32[]{:S(2)}, u32[]{:S(2)}) collective-permute-start(bf16[512,1024]{1,0:T(8,128)(2,1)S(1)} %collective-permute-done.2), channel_id=1, source_target_pairs={{0,2},{2,4},{4,6},{6,8},{8,10},{10,12},{12,14},{14,0},{1,3},{3,5},... | collective-permute-start | bytes 3145736 | tf_op jit(solution)/shard_map/ppermute | solution.py:20
  196.1 23.3 %collective-permute-start.4 = (bf16[512,1024]{1,0:T(8,128)(2,1)}, bf16[512,1024]{1,0:T(8,128)(2,1)}, u32[]{:S(2)}, u32[]{:S(2)}) collective-permute-start(bf16[512,1024]{1,0:T(8,128)(2,1)} %collective-permute-done.3), channel_id=1, source_target_pairs={{0,2},{2,4},{4,6},{6,8},{8,10},{10,12},{12,14},{14,0},{1,3},{3,5},... | collective-permute-start | bytes 3145736 | tf_op jit(solution)/shard_map/ppermute | solution.py:20
  196.1 102.1 %all-gather.8.cloned.1.call-start = ((), (), s32[]{:S(2)}) async-start(), calls=%async_computation.3 | async-start | bytes 2359296 | tf_op jit(solution)/shard_map/all_gather | solution.py:29
  219.4 23.3 %collective-permute-start.5 = (bf16[512,1024]{1,0:T(8,128)(2,1)}, bf16[512,1024]{1,0:T(8,128)(2,1)}, u32[]{:S(2)}, u32[]{:S(2)}) collective-permute-start(bf16[512,1024]{1,0:T(8,128)(2,1)} %collective-permute-done.4), channel_id=1, source_target_pairs={{0,2},{2,4},{4,6},{6,8},{8,10},{10,12},{12,14},{14,0},{1,3},{3,5},... | collective-permute-start | bytes 3145736 | tf_op jit(solution)/shard_map/ppermute | solution.py:20
  242.7 28.1 %collective-permute-start.6 = (bf16[512,1024]{1,0:T(8,128)(2,1)}, bf16[512,1024]{1,0:T(8,128)(2,1)}, u32[]{:S(2)}, u32[]{:S(2)}) collective-permute-start(bf16[512,1024]{1,0:T(8,128)(2,1)} %collective-permute-done.5), channel_id=1, source_target_pairs={{0,2},{2,4},{4,6},{6,8},{8,10},{10,12},{12,14},{14,0},{1,3},{3,5},... | collective-permute-start | bytes 3145736 | tf_op jit(solution)/shard_map/ppermute | solution.py:20
  242.8 145.0 %reduce-scatter.2.cloned.1.call-start = ((), (), s32[]{:S(2)}) async-start(), calls=%async_computation.4 | async-start | bytes 4718592 | tf_op jit(solution)/shard_map/reduce_scatter | solution.py:33
  242.9 42.5 %copy-start.6 = (bf16[512,1024]{1,0:T(8,128)(2,1)S(1)}, bf16[512,1024]{1,0:T(8,128)(2,1)}, u32[]{:S(2)}) copy-start(bf16[512,1024]{1,0:T(8,128)(2,1)} %copy-done.5) | copy-start | bytes 3145732
  242.9 42.6 %copy-start.4 = (bf16[512,1024]{1,0:T(8,128)(2,1)S(1)}, bf16[512,1024]{1,0:T(8,128)(2,1)}, u32[]{:S(2)}) copy-start(bf16[512,1024]{1,0:T(8,128)(2,1)} %copy-done.3) | copy-start | bytes 3145732
  242.9 42.7 %copy-start.2 = (bf16[512,1024]{1,0:T(8,128)(2,1)S(1)}, bf16[512,1024]{1,0:T(8,128)(2,1)}, u32[]{:S(2)}) copy-start(bf16[512,1024]{1,0:T(8,128)(2,1)} %copy-done.1) | copy-start | bytes 3145732
  245.2 40.6 %copy-start.7 = (bf16[256,4096]{1,0:T(8,128)(2,1)S(1)}, bf16[256,4096]{1,0:T(8,128)(2,1)}, u32[]{:S(2)}) copy-start(bf16[256,4096]{1,0:T(8,128)(2,1)} %all-gather.6.cloned.1.call-done) | copy-start | bytes 6291460
  245.2 40.6 %copy-start.10 = (f32[4096]{0:T(1024)S(1)}, f32[4096]{0:T(1024)}, u32[]{:S(2)}) copy-start(f32[4096]{0:T(1024)} %param.7) | copy-start | bytes 49156
  280.0 8.9 %copy-start.9 = (bf16[256,1024]{1,0:T(8,128)(2,1)S(1)}, bf16[256,1024]{1,0:T(8,128)(2,1)}, u32[]{:S(2)}) copy-start(bf16[256,1024]{1,0:T(8,128)(2,1)} %param.11) | copy-start | bytes 1572868
  288.2 0.8 copy-start.8
Sparse Core Ops, SparseCore 0:
  12.5 75.8 all-gather.3
Sparse Core Ops, SparseCore 1:
  196.2 11.8 all-gather.5
  242.9 55.4 all-gather.7
  301.8 86.0 reduce-scatter.1
